TPU v7x, 128 devices: a whole 4x4x4 slice. The times are simulated.
128 devices in a mesh: ctx: 32 (over y, z, x_lo), seq: 2 (over core), fsdp: 2 (over x_hi).
Axes of the slice: x: 4 (x_hi: 2, x_lo: 2; x = x_hi * 2 + x_lo), y: 4, z: 4, core: 2. Of those that a mesh axis runs over, the one named last changes fastest.
Arguments:
- tokens: bfloat16 [4, 4096, 768], P(('seq', 'fsdp'), 'ctx'), may hold values from -6 to 6
- cotangent: bfloat16 [4, 4096, 768], P(('seq', 'fsdp'), 'ctx'), may hold values from -6 to 6
- w_query: bfloat16 [768, 768], P('fsdp'), may hold values from -0.21875 to 0.21875
- w_key: bfloat16 [768, 768], P('fsdp'), may hold values from -0.21875 to 0.21875
- w_value: bfloat16 [768, 768], P('fsdp'), may hold values from -0.21875 to 0.21875
- w_output: bfloat16 [768, 768], P('fsdp'), may hold values from -6 to 6
- b_query: bfloat16 [768], P('fsdp'), may hold values from -1.5 to 1.5
- b_value: bfloat16 [768], P('fsdp'), may hold values from -0.15625 to 0.15625
- b_output: bfloat16 [768], P('fsdp'), may hold values from -1.5 to 1.5
- first_gain: bfloat16 [768], P('fsdp'), may hold values from 0.5 to 1.5
- first_shift: bfloat16 [768], P('fsdp'), may hold values from -1.5 to 1.5
- w_inner: bfloat16 [768, 3072], P('fsdp'), may hold values from -0.21875 to 0.21875
- b_inner: bfloat16 [3072], P('fsdp'), may hold values from -1.5 to 1.5
- w_outer: bfloat16 [3072, 768], P('fsdp'), may hold values from -0.109375 to 0.109375
- b_outer: bfloat16 [768], P('fsdp'), may hold values from -1.5 to 1.5
- second_gain: bfloat16 [768], P('fsdp'), may hold values from 0.5 to 1.5
- second_shift: bfloat16 [768], P('fsdp'), may hold values from -1.5 to 1.5
Outputs:
- layer_out: bfloat16 [4, 4096, 768], P(('seq', 'fsdp'), 'ctx')
- tokens_grad: float32 [4, 4096, 768], P(('seq', 'fsdp'), 'ctx')
- w_query_grad: float32 [768, 768], P('fsdp')
- w_key_grad: float32 [768, 768], P('fsdp')
- w_value_grad: float32 [768, 768], P('fsdp')
- w_output_grad: float32 [768, 768], P('fsdp')
- b_query_grad: float32 [768], P('fsdp')
- b_value_grad: float32 [768], P('fsdp')
- b_output_grad: float32 [768], P('fsdp')
- first_gain_grad: float32 [768], P('fsdp')
- first_shift_grad: float32 [768], P('fsdp')
- w_inner_grad: float32 [768, 3072], P('fsdp')
- b_inner_grad: float32 [3072], P('fsdp')
- w_outer_grad: float32 [3072, 768], P('fsdp')
- b_outer_grad: float32 [768], P('fsdp')
- second_gain_grad: float32 [768], P('fsdp')
- second_shift_grad: float32 [768], P('fsdp')
All inputs are finite; a program needn't handle non-finite values.
Results may differ from a plain program's by a relative error of at most 0.022.
Values may be sent and summed in bfloat16 or wider, within the bound.
A program may use at most 192 MiB of HBM per device.

v0:
```python
import functools
import jax
import jax.numpy as jnp
from jax import lax
from jax.sharding import PartitionSpec as P

HEADS = 12
HEAD_DIM = 64
epsilon = 1e-12


def product(left, right):
    return jnp.dot(left, right, preferred_element_type=jnp.float32)


def product_left(left, right):
    return lax.dot_general(
        left, right, (((0,), (0,)), ((), ())), preferred_element_type=jnp.float32
    )


def product_right(left, right):
    return lax.dot_general(
        left, right, (((1,), (1,)), ((), ())), preferred_element_type=jnp.float32
    )


def layer_norm(hidden, gain, shift):
    centred = hidden - jnp.mean(hidden, axis=-1, keepdims=True)
    inverse = lax.rsqrt(jnp.mean(centred * centred, axis=-1, keepdims=True) + epsilon)
    normal = centred * inverse
    return (normal * gain + shift, normal, inverse)


def norm_back(grad, normal, inverse, gain):
    scaled = grad * gain
    centre = jnp.mean(scaled, axis=-1, keepdims=True)
    along = jnp.mean(scaled * normal, axis=-1, keepdims=True)
    return inverse * (scaled - centre - normal * along)


def group_slice(array, index):
    columns = 2 * HEAD_DIM
    piece = lax.dynamic_slice_in_dim(array, index * columns, columns, 2)
    return piece.reshape(piece.shape[0], piece.shape[1], 2, HEAD_DIM)


def scores_of(query, keys):
    return jnp.einsum(
        "sqhd,skhd->shqk", query, keys, preferred_element_type=jnp.float32
    ) * HEAD_DIM ** (-0.5)


def flatten_group(array):
    return array.reshape(array.shape[0], array.shape[1], 2 * HEAD_DIM)


def to_rows(stacked):
    groups, seqs, count, columns = stacked.shape
    return stacked.transpose(1, 2, 0, 3).reshape(seqs * count, groups * columns)


def local(
    tokens,
    cotangent,
    w_query,
    w_key,
    w_value,
    w_output,
    b_query,
    b_value,
    b_output,
    first_gain,
    first_shift,
    w_inner,
    b_inner,
    w_outer,
    b_outer,
    second_gain,
    second_shift,
):
    seqs, block, width = tokens.shape
    rows = seqs * block
    indices = jnp.arange(HEADS // 2)
    scale = HEAD_DIM ** (-0.5)
    w_query, w_key, w_value, w_output, b_query, b_value, b_output, first_gain, first_shift = (
        lax.all_gather(w_query, "fsdp", axis=0, tiled=True),
        lax.all_gather(w_key, "fsdp", axis=0, tiled=True),
        lax.all_gather(w_value, "fsdp", axis=0, tiled=True),
        lax.all_gather(w_output, "fsdp", axis=0, tiled=True),
        lax.all_gather(b_query, "fsdp", axis=0, tiled=True),
        lax.all_gather(b_value, "fsdp", axis=0, tiled=True),
        lax.all_gather(b_output, "fsdp", axis=0, tiled=True),
        lax.all_gather(first_gain, "fsdp", axis=0, tiled=True),
        lax.all_gather(first_shift, "fsdp", axis=0, tiled=True),
    )
    flat = tokens.reshape(rows, width)
    query = (product(flat, w_query) + b_query).astype(jnp.bfloat16).reshape(seqs, block, width)
    keys = product(flat, w_key).astype(jnp.bfloat16).reshape(seqs, block, width)
    values = (product(flat, w_value) + b_value).astype(jnp.bfloat16).reshape(seqs, block, width)
    keys_all, values_all = (
        lax.all_gather(keys, "ctx", axis=1, tiled=True),
        lax.all_gather(values, "ctx", axis=1, tiled=True),
    )

    def forward_group(index):
        scores = scores_of(group_slice(query, index), group_slice(keys_all, index))
        top = jnp.max(scores, axis=-1, keepdims=True)
        weights = jnp.exp(scores - top)
        total = jnp.sum(weights, axis=-1, keepdims=True)
        probs = (weights / total).astype(jnp.bfloat16)
        mixed = jnp.einsum(
            "shqk,skhd->sqhd",
            probs,
            group_slice(values_all, index),
            preferred_element_type=jnp.float32,
        )
        return (flatten_group(mixed), (top + jnp.log(total))[..., 0])

    mixed, logsum = lax.map(forward_group, indices)
    attended = to_rows(mixed).astype(jnp.bfloat16)
    first_in = flat.astype(jnp.float32) + product(attended, w_output) + b_output
    normed, first_normal, first_inverse = layer_norm(first_in, first_gain, first_shift)
    normed_low = normed.astype(jnp.bfloat16)
    w_inner, b_inner, w_outer, b_outer, second_gain, second_shift = (
        lax.all_gather(w_inner, "fsdp", axis=0, tiled=True),
        lax.all_gather(b_inner, "fsdp", axis=0, tiled=True),
        lax.all_gather(w_outer, "fsdp", axis=0, tiled=True),
        lax.all_gather(b_outer, "fsdp", axis=0, tiled=True),
        lax.all_gather(second_gain, "fsdp", axis=0, tiled=True),
        lax.all_gather(second_shift, "fsdp", axis=0, tiled=True),
    )
    gelu_exact = functools.partial(jax.nn.gelu, approximate=False)
    inner = product(normed_low, w_inner) + b_inner
    active = gelu_exact(inner).astype(jnp.bfloat16)
    second_in = normed + product(active, w_outer) + b_outer
    layer_out, second_normal, second_inverse = layer_norm(second_in, second_gain, second_shift)
    grad_out = cotangent.reshape(rows, width).astype(jnp.float32)
    second_scale = jnp.sum(grad_out * second_normal, axis=0)
    second_offset = jnp.sum(grad_out, axis=0)
    grad_second = norm_back(grad_out, second_normal, second_inverse, second_gain)
    outer_low = grad_second.astype(jnp.bfloat16)
    outer_matrix = product_left(active, outer_low)
    outer_bias = jnp.sum(outer_low.astype(jnp.float32), axis=0)
    slope = jax.vjp(gelu_exact, inner)[1](product_right(outer_low, w_outer))[0]
    inner_low = slope.astype(jnp.bfloat16)
    inner_matrix = product_left(normed_low, inner_low)
    inner_bias = jnp.sum(inner_low.astype(jnp.float32), axis=0)
    grad_normed = grad_second + product_right(inner_low, w_inner)
    first_scale = jnp.sum(grad_normed * first_normal, axis=0)
    first_offset = jnp.sum(grad_normed, axis=0)
    grad_first = norm_back(grad_normed, first_normal, first_inverse, first_gain)
    branch_low = grad_first.astype(jnp.bfloat16)
    output_matrix = product_left(attended, branch_low)
    output_bias = jnp.sum(branch_low.astype(jnp.float32), axis=0)
    upstream = product_right(branch_low, w_output).astype(jnp.bfloat16).reshape(seqs, block, width)

    def backward_group(pair):
        index, group_logsum = pair
        query_part = group_slice(query, index)
        keys_part = group_slice(keys_all, index)
        values_part = group_slice(values_all, index)
        upstream_part = group_slice(upstream, index)
        probs = jnp.exp(scores_of(query_part, keys_part) - group_logsum[..., None])
        prob_grads = jnp.einsum(
            "sqhd,skhd->shqk", upstream_part, values_part, preferred_element_type=jnp.float32
        )
        row_dot = jnp.sum(probs * prob_grads, axis=-1, keepdims=True)
        score_low = (probs * (prob_grads - row_dot)).astype(jnp.bfloat16)
        query_grad = (
            jnp.einsum("shqk,skhd->sqhd", score_low, keys_part, preferred_element_type=jnp.float32)
            * scale
        )
        key_grad = (
            jnp.einsum("shqk,sqhd->skhd", score_low, query_part, preferred_element_type=jnp.float32)
            * scale
        )
        value_grad = jnp.einsum(
            "shqk,sqhd->skhd",
            probs.astype(jnp.bfloat16),
            upstream_part,
            preferred_element_type=jnp.float32,
        )
        return (flatten_group(query_grad), flatten_group(key_grad), flatten_group(value_grad))

    query_grads, key_terms, value_terms = lax.map(backward_group, (indices, logsum))
    key_grads, value_grads = (
        lax.psum_scatter(
            key_terms.astype(jnp.bfloat16), "ctx", scatter_dimension=2, tiled=True
        ).astype(jnp.float32),
        lax.psum_scatter(
            value_terms.astype(jnp.bfloat16), "ctx", scatter_dimension=2, tiled=True
        ).astype(jnp.float32),
    )
    query_low = to_rows(query_grads).astype(jnp.bfloat16)
    key_low = to_rows(key_grads).astype(jnp.bfloat16)
    value_low = to_rows(value_grads).astype(jnp.bfloat16)
    query_matrix = product_left(flat, query_low)
    query_bias = jnp.sum(query_low.astype(jnp.float32), axis=0)
    keys_matrix = product_left(flat, key_low)
    value_matrix = product_left(flat, value_low)
    value_bias = jnp.sum(value_low.astype(jnp.float32), axis=0)
    tokens_grad = (
        grad_first
        + product_right(query_low, w_query)
        + product_right(key_low, w_key)
        + product_right(value_low, w_value)
    )
    (
        query_matrix,
        keys_matrix,
        value_matrix,
        output_matrix,
        query_bias,
        value_bias,
        output_bias,
        first_scale,
        first_offset,
        inner_matrix,
        inner_bias,
        outer_matrix,
        outer_bias,
        second_scale,
        second_offset,
    ) = (
        lax.psum_scatter(
            query_matrix.astype(jnp.bfloat16), "fsdp", scatter_dimension=0, tiled=True
        ).astype(jnp.float32),
        lax.psum_scatter(
            keys_matrix.astype(jnp.bfloat16), "fsdp", scatter_dimension=0, tiled=True
        ).astype(jnp.float32),
        lax.psum_scatter(
            value_matrix.astype(jnp.bfloat16), "fsdp", scatter_dimension=0, tiled=True
        ).astype(jnp.float32),
        lax.psum_scatter(
            output_matrix.astype(jnp.bfloat16), "fsdp", scatter_dimension=0, tiled=True
        ).astype(jnp.float32),
        lax.psum_scatter(
            query_bias.astype(jnp.bfloat16), "fsdp", scatter_dimension=0, tiled=True
        ).astype(jnp.float32),
        lax.psum_scatter(
            value_bias.astype(jnp.bfloat16), "fsdp", scatter_dimension=0, tiled=True
        ).astype(jnp.float32),
        lax.psum_scatter(
            output_bias.astype(jnp.bfloat16), "fsdp", scatter_dimension=0, tiled=True
        ).astype(jnp.float32),
        lax.psum_scatter(
            first_scale.astype(jnp.bfloat16), "fsdp", scatter_dimension=0, tiled=True
        ).astype(jnp.float32),
        lax.psum_scatter(
            first_offset.astype(jnp.bfloat16), "fsdp", scatter_dimension=0, tiled=True
        ).astype(jnp.float32),
        lax.psum_scatter(
            inner_matrix.astype(jnp.bfloat16), "fsdp", scatter_dimension=0, tiled=True
        ).astype(jnp.float32),
        lax.psum_scatter(
            inner_bias.astype(jnp.bfloat16), "fsdp", scatter_dimension=0, tiled=True
        ).astype(jnp.float32),
        lax.psum_scatter(
            outer_matrix.astype(jnp.bfloat16), "fsdp", scatter_dimension=0, tiled=True
        ).astype(jnp.float32),
        lax.psum_scatter(
            outer_bias.astype(jnp.bfloat16), "fsdp", scatter_dimension=0, tiled=True
        ).astype(jnp.float32),
        lax.psum_scatter(
            second_scale.astype(jnp.bfloat16), "fsdp", scatter_dimension=0, tiled=True
        ).astype(jnp.float32),
        lax.psum_scatter(
            second_offset.astype(jnp.bfloat16), "fsdp", scatter_dimension=0, tiled=True
        ).astype(jnp.float32),
    )
    finals = lax.psum(
        (
            query_matrix,
            keys_matrix,
            value_matrix,
            output_matrix,
            query_bias,
            value_bias,
            output_bias,
            first_scale,
            first_offset,
            inner_matrix,
            inner_bias,
            outer_matrix,
            outer_bias,
            second_scale,
            second_offset,
        ),
        ("ctx", "seq"),
    )
    return (
        layer_out.astype(jnp.bfloat16).reshape(seqs, block, width),
        tokens_grad.reshape(seqs, block, width),
    ) + tuple(finals)


def solution(mesh):
    return jax.shard_map(
        local,
        mesh=mesh,
        in_specs=(
            P(("seq", "fsdp"), "ctx", None),
            P(("seq", "fsdp"), "ctx", None),
            P("fsdp", None),
            P("fsdp", None),
            P("fsdp", None),
            P("fsdp", None),
            P("fsdp"),
            P("fsdp"),
            P("fsdp"),
            P("fsdp"),
            P("fsdp"),
            P("fsdp", None),
            P("fsdp"),
            P("fsdp", None),
            P("fsdp"),
            P("fsdp"),
            P("fsdp"),
        ),
        out_specs=(
            P(("seq", "fsdp"), "ctx", None),
            P(("seq", "fsdp"), "ctx", None),
            P("fsdp", None),
            P("fsdp", None),
            P("fsdp", None),
            P("fsdp", None),
            P("fsdp"),
            P("fsdp"),
            P("fsdp"),
            P("fsdp"),
            P("fsdp"),
            P("fsdp", None),
            P("fsdp"),
            P("fsdp", None),
            P("fsdp"),
            P("fsdp"),
            P("fsdp"),
        ),
        check_vma=False,
    )
```

profile of v0, /device:TPU:0, one launch (start us, length us, event | category | flops | bytes accessed | tf_op | source)
XLA Modules:
  0.0 1809.2 jit_solution(1213545254661435694)
XLA Ops:
  15.4 23.6 %all-gather.20.cloned.1.call-done = bf16[768,768]{1,0:T(8,128)(2,1)} async-done(((bf16[384,768]{1,0:T(8,128)(2,1)}), bf16[768,768]{1,0:T(8,128)(2,1)}) %all-gather.20.cloned.1.call-update) | async-done | bytes 1179664 | tf_op jit(solution)/shard_map/all_gather | solution.py:89
  41.3 25.6 %all-gather.24.cloned.1.call-done = bf16[768,768]{1,0:T(8,128)(2,1)} async-done(((bf16[384,768]{1,0:T(8,128)(2,1)}), bf16[768,768]{1,0:T(8,128)(2,1)}) %all-gather.24.cloned.1.call-update) | async-done | bytes 1179664 | tf_op jit(solution)/shard_map/all_gather | solution.py:88
  120.5 150.1 %all-gather.32.cloned.1.call-done = bf16[4096,768]{1,0:T(8,128)(2,1)} async-done(((bf16[128,768]{1,0:T(8,128)(2,1)}), bf16[4096,768]{1,0:T(8,128)(2,1)}) %all-gather.32.cloned.1.call-update) | async-done | bytes 6291472 | tf_op jit(solution)/shard_map/all_gather | solution.py:103
  270.5 8.7 copy.44
  279.2 166.5 %all-gather.34.cloned.1.call-done = bf16[4096,768]{1,0:T(8,128)(2,1)} async-done(((bf16[128,768]{1,0:T(8,128)(2,1)}), bf16[4096,768]{1,0:T(8,128)(2,1)}) %all-gather.34.cloned.1.call-update) | async-done | bytes 6291472 | tf_op jit(solution)/shard_map/all_gather | solution.py:102
  445.8 8.6 copy.46
  454.4 33.8 %while.26 = (s32[]{:T(128)}, bf16[6,1,128,128]{2,3,1,0:T(8,128)(2,1)S(1)}, f32[6,1,2,128]{3,2,1,0:T(2,128)S(1)}, s32[6]{0:T(128)S(1)}, bf16[1,4096,768]{1,2,0:T(...) while((s32[]{:T(128)}, ...), condition=%wide.region_3.4_spmd, body=%wide.region_0.3_spmd.sunk | while | flops 275775232 | bytes 19079360 | solution.py:120
  490.3 49.7 %all-gather.28.cloned.1.call-done = bf16[768,3072]{1,0:T(8,128)(2,1)} async-done(((bf16[384,3072]{1,0:T(8,128)(2,1)}), bf16[768,3072]{1,0:T(8,128)(2,1)}) %all-gather.28.cloned.1.call-update) | async-done | bytes 4718608 | tf_op jit(solution)/shard_map/all_gather | solution.py:126
  548.4 59.5 %all-gather.30.cloned.1.call-done = bf16[3072,768]{1,0:T(8,128)(2,1)} async-done(((bf16[1536,768]{1,0:T(8,128)(2,1)}), bf16[3072,768]{1,0:T(8,128)(2,1)}) %all-gather.30.cloned.1.call-update) | async-done | bytes 4718608 | tf_op jit(solution)/shard_map/all_gather | solution.py:128
  619.1 72.0 %while.27 = (s32[]{:T(128)}, bf16[6,1,128,128]{2,3,1,0:T(8,128)(2,1)S(1)}, bf16[6,1,4096,128]{2,3,1,0:T(8,128)(2,1)}, bf16[6,1,4096,128]{2,3,1,0:T(8,128)(2,1)},...) while((s32[]{:T(128)}, ...), condition=%wide.region_14.15_spmd, body=%wide.region_12.14_spmd.sunk | while | flops 680558336 | bytes 47093020 | solution.py:186
  691.1 27.8 %copy.54 = bf16[6,1,4096,128]{3,1,0,2:T(2,128)(2,1)} copy(bf16[6,1,4096,128]{2,3,1,0:T(8,128)(2,1)} %get-tuple-element.112) | data formatting | bytes 12582912
  718.9 110.1 %bitcast_reduce_fusion.1 = bf16[4096,6,128]{2,1,0:T(8,128)(2,1)} fusion(bf16[6,1,4096,128]{3,1,0,2:T(2,128)(2,1)} %copy.54), kind=kLoop, calls=%fused_computation.29 | loop fusion | bytes 12582912
  836.8 27.9 %copy.56 = bf16[6,1,4096,128]{3,1,0,2:T(2,128)(2,1)} copy(bf16[6,1,4096,128]{2,3,1,0:T(8,128)(2,1)} %get-tuple-element.113) | data formatting | bytes 12582912
  864.6 110.0 %bitcast_reduce_fusion = bf16[4096,6,128]{2,1,0:T(8,128)(2,1)} fusion(bf16[6,1,4096,128]{3,1,0,2:T(2,128)(2,1)} %copy.56), kind=kLoop, calls=%fused_computation.28 | loop fusion | bytes 12582912
  995.5 21.0 %reduce-scatter.25.cloned.1.call-done = bf16[128,768]{1,0:T(8,128)(2,1)} async-done(((bf16[4096,768]{1,0:T(8,128)(2,1)}), bf16[128,768]{1,0:T(8,128)(2,1)}) %reduce-scatter.25.cloned.1.call-update) | async-done | bytes 196624
  1020.3 176.3 %reduce-scatter.27.cloned.1.call-done = bf16[128,768]{1,0:T(8,128)(2,1)} async-done(((bf16[4096,768]{1,0:T(8,128)(2,1)}), bf16[128,768]{1,0:T(8,128)(2,1)}) %reduce-scatter.27.cloned.1.call-update) | async-done | bytes 196624
  1203.8 18.1 reduce-scatter.29.cloned.1.call-done
  1223.3 26.8 %reduce-scatter.19.cloned.1.call-done = bf16[384,768]{1,0:T(8,128)(2,1)} async-done(((bf16[768,768]{1,0:T(8,128)(2,1)}), bf16[384,768]{1,0:T(8,128)(2,1)}) %reduce-scatter.19.cloned.1.call-update) | async-done | bytes 589840 | tf_op jit(solution)/shard_map/reduce_scatter | solution.py:235
  1250.1 66.5 %reduce-scatter.21.cloned.1.call-done = bf16[384,3072]{1,0:T(8,128)(2,1)} async-done(((bf16[768,3072]{1,0:T(8,128)(2,1)}), bf16[384,3072]{1,0:T(8,128)(2,1)}) %reduce-scatter.21.cloned.1.call-update) | async-done | bytes 2359312 | tf_op jit(solution)/shard_map/reduce_scatter | solution.py:253
  1316.5 66.5 %reduce-scatter.23.cloned.1.call-done = bf16[1536,768]{1,0:T(8,128)(2,1)} async-done(((bf16[3072,768]{1,0:T(8,128)(2,1)}), bf16[1536,768]{1,0:T(8,128)(2,1)}) %reduce-scatter.23.cloned.1.call-update) | async-done | bytes 2359312 | tf_op jit(solution)/shard_map/reduce_scatter | solution.py:259
  1383.2 8.6 all-reduce.10
  1395.3 15.8 reduce-scatter.31.cloned.1.call-done
  1412.4 26.8 %reduce-scatter.33.cloned.1.call-done = bf16[384,768]{1,0:T(8,128)(2,1)} async-done(((bf16[768,768]{1,0:T(8,128)(2,1)}), bf16[384,768]{1,0:T(8,128)(2,1)}) %reduce-scatter.33.cloned.1.call-update) | async-done | bytes 589840
  1440.6 356.2 %all-reduce.12 = (f32[384,768]{0,1:T(8,128)}, f32[384,768]{0,1:T(8,128)}, f32[384,768]{0,1:T(8,128)S(1)}, f32[384,768]{1,0:T(8,128)}, f32[384]{0:T(512)}, /*inde...) all-reduce(bf16[384,768]{0,1:T(8,128)(2,1)S(1)} %copy.59, ...), channel_id=1, replica_groups=mesh['ctx'=32,'seq'=2,'fsdp'=2] {'ctx','seq'}, use_global_device_ids=true, to_apply=%region_18.19 | all-reduce | flops 3543552 | bytes 21270528 | tf_op jit(solution)/shard_map/psum | solution.py:272
  (359 shorter events, 233.4 us)
Async XLA Ops:
  7.2 31.8 %copy-start = (bf16[1,128,768]{2,1,0:T(8,128)(2,1)S(1)}, bf16[1,128,768]{2,1,0:T(8,128)(2,1)}, u32[]{:S(2)}) copy-start(bf16[1,128,768]{2,1,0:T(8,128)(2,1)} %param.21) | copy-start | bytes 589828
  7.2 31.8 %all-gather.20.cloned.1.call-start = ((), (), s32[]{:S(2)}) async-start(), calls=%async_computation.8 | async-start | bytes 1769472 | tf_op jit(solution)/shard_map/all_gather | solution.py:89
  7.9 59.0 %all-gather.24.cloned.1.call-start = ((), (), s32[]{:S(2)}) async-start(), calls=%async_computation.10 | async-start | bytes 1769472 | tf_op jit(solution)/shard_map/all_gather | solution.py:88
  8.7 110.0 %all-gather.22.cloned.1.call-start = ((), (), s32[]{:S(2)}) async-start(), calls=%async_computation.9 | async-start | bytes 1769472 | tf_op jit(solution)/shard_map/all_gather | solution.py:87
  9.4 261.1 %all-gather.32.cloned.1.call-start = ((), (), s32[]{:S(2)}) async-start(), calls=%async_computation.17 | async-start | bytes 6488064 | tf_op jit(solution)/shard_map/all_gather | solution.py:103
  41.3 404.5 %all-gather.34.cloned.1.call-start = ((), (), s32[]{:S(2)}) async-start(), calls=%async_computation.18 | async-start | bytes 6488064 | tf_op jit(solution)/shard_map/all_gather | solution.py:102
  69.2 419.0 %all-gather.26.cloned.1.call-start = ((), (), s32[]{:S(2)}) async-start(), calls=%async_computation.11 | async-start | bytes 1769472 | tf_op jit(solution)/shard_map/all_gather | solution.py:90
  69.8 470.2 %all-gather.28.cloned.1.call-start = ((), (), s32[]{:S(2)}) async-start(), calls=%async_computation.12 | async-start | bytes 7077888 | tf_op jit(solution)/shard_map/all_gather | solution.py:126
  70.6 30.3 %copy-start.22 = (bf16[384]{0:T(512)(128)(2,1)S(1)}, bf16[384]{0:T(512)(128)(2,1)}, u32[]{:S(2)}) copy-start(bf16[384]{0:T(512)(128)(2,1)} %param.30) | copy-start | bytes 2308
  70.6 36.2 %copy-start.23 = (bf16[384]{0:T(512)(128)(2,1)S(1)}, bf16[384]{0:T(512)(128)(2,1)}, u32[]{:S(2)}) copy-start(bf16[384]{0:T(512)(128)(2,1)} %param.36) | copy-start | bytes 2308
  70.6 42.1 %copy-start.24 = (bf16[384]{0:T(512)(128)(2,1)S(1)}, bf16[384]{0:T(512)(128)(2,1)}, u32[]{:S(2)}) copy-start(bf16[384]{0:T(512)(128)(2,1)} %param.37) | copy-start | bytes 2308
  70.7 537.2 %all-gather.30.cloned.1.call-start = ((), (), s32[]{:S(2)}) async-start(), calls=%async_computation.13 | async-start | bytes 7077888 | tf_op jit(solution)/shard_map/all_gather | solution.py:128
  71.4 945.1 %reduce-scatter.25.cloned.1.call-start = ((), (), s32[]{:S(2)}) async-start(), calls=%async_computation.19 | async-start | bytes 6488064
  488.2 60.2 %copy-start.7 = (bf16[6,1,128,128]{2,3,1,0:T(8,128)(2,1)}, bf16[6,1,128,128]{2,3,1,0:T(8,128)(2,1)S(1)}, u32[]{:S(2)}) copy-start(bf16[6,1,128,128]{2,3,1,0:T(8,128)(2,1)S(1)} %get-tuple-element.109) | copy-start | bytes 589828
  836.7 359.9 %reduce-scatter.27.cloned.1.call-start = ((), (), s32[]{:S(2)}) async-start(), calls=%async_computation.20 | async-start | bytes 6488064
  982.3 239.6 %reduce-scatter.29.cloned.1.call-start = ((), (), s32[]{:S(2)}) async-start(), calls=%async_computation.21 | async-start | bytes 1769472
  986.3 263.8 %reduce-scatter.19.cloned.1.call-start = ((), (), s32[]{:S(2)}) async-start(), calls=%async_computation.14 | async-start | bytes 1769472 | tf_op jit(solution)/shard_map/reduce_scatter | solution.py:235
  988.0 328.5 %reduce-scatter.21.cloned.1.call-start = ((), (), s32[]{:S(2)}) async-start(), calls=%async_computation.15 | async-start | bytes 7077888 | tf_op jit(solution)/shard_map/reduce_scatter | solution.py:253
  991.8 391.2 %reduce-scatter.23.cloned.1.call-start = ((), (), s32[]{:S(2)}) async-start(), calls=%async_computation.16 | async-start | bytes 7077888 | tf_op jit(solution)/shard_map/reduce_scatter | solution.py:259
  995.5 415.5 %reduce-scatter.31.cloned.1.call-start = ((), (), s32[]{:S(2)}) async-start(), calls=%async_computation.22 | async-start | bytes 1769472
  1020.3 418.9 %reduce-scatter.33.cloned.1.call-start = ((), (), s32[]{:S(2)}) async-start(), calls=%async_computation.23 | async-start | bytes 1769472
  1202.5 189.9 %copy-start.2 = (bf16[768,768]{1,0:T(8,128)(2,1)S(1)}, bf16[768,768]{1,0:T(8,128)(2,1)}, u32[]{:S(2)}) copy-start(bf16[768,768]{1,0:T(8,128)(2,1)} %all-gather.24.cloned.1.call-done) | copy-start | bytes 3538948
  1203.8 188.7 %copy-start.10 = (bf16[6,1,128,128]{2,3,1,0:T(8,128)(2,1)S(1)}, bf16[6,1,128,128]{2,3,1,0:T(8,128)(2,1)}, u32[]{:S(2)}) copy-start(bf16[6,1,128,128]{2,3,1,0:T(8,128)(2,1)} %copy-done.9) | copy-start | bytes 589828
  1203.8 190.2 %copy-start.1 = (bf16[768,768]{1,0:T(8,128)(2,1)S(1)}, bf16[768,768]{1,0:T(8,128)(2,1)}, u32[]{:S(2)}) copy-start(bf16[768,768]{1,0:T(8,128)(2,1)} %all-gather.20.cloned.1.call-done) | copy-start | bytes 3538948
  (34 other events, 125.0 us)
Sparse Core Ops, SparseCore 0:
  9.7 29.2 all-gather.19
  40.6 26.2 all-gather.23
  68.6 26.3 all-gather.21
  97.1 173.4 all-gather.31
  272.6 173.1 all-gather.33
  447.3 24.7 all-gather.25
  473.7 66.2 all-gather.27
  541.6 66.1 all-gather.29
  836.8 179.6 reduce-scatter.24
  1018.8 177.7 reduce-scatter.26
  1199.5 22.3 reduce-scatter.28
  1224.8 25.2 reduce-scatter.18
  1253.0 63.4 reduce-scatter.20
  1319.5 63.4 reduce-scatter.22
  1385.8 25.2 reduce-scatter.30
  1413.9 25.2 reduce-scatter.32
where the time goes:
time: 1820 us; the launch traced here: 1810 us
  waiting for transfers between devices  897 us (49%)
  blocking collectives  417 us (23%)
  local copies, waits for them, and re-layouts  382 us (21%)
  matrix products  74.2 us (4%)
    psum x1, blocking collectives, local(): lax.psum((query_matrix, keys_matrix, value_matrix, output_matrix, query_b...  356 us
    unnamed x89, local copies, waits for them, and re-layouts  312 us
    unnamed x21, waiting for transfers between devices  262 us
    all_gather x1, waiting for transfers between devices, local(): lax.all_gather(keys, 'ctx', axis=1, tiled=True)  167 us
    all_gather x1, waiting for transfers between devices, local(): lax.all_gather(values, 'ctx', axis=1, tiled=True)  150 us
    reduce_scatter x1, waiting for transfers between devices, local(): lax.psum_scatter(outer_matrix.astype(jnp.bfloat16), 'fsdp', scatter_dimen...  66.5 us
    reduce_scatter x1, waiting for transfers between devices, local(): lax.psum_scatter(inner_matrix.astype(jnp.bfloat16), 'fsdp', scatter_dimen...  66.5 us
    all_gather x1, waiting for transfers between devices, local(): lax.all_gather(w_outer, 'fsdp', axis=0, tiled=True)  59.5 us
  transfers between devices with their start and end apart: 16, of which 14 were waited for; matrix products, arithmetic and copies ran while one was open for 13% of the time, Pallas kernels for 0%

commit v1 on v0

--- a/solution.py
+++ b/solution.py
@@ -269,26 +269,25 @@
             second_offset.astype(jnp.bfloat16), "fsdp", scatter_dimension=0, tiled=True
         ).astype(jnp.float32),
     )
-    finals = lax.psum(
-        (
-            query_matrix,
-            keys_matrix,
-            value_matrix,
-            output_matrix,
-            query_bias,
-            value_bias,
-            output_bias,
-            first_scale,
-            first_offset,
-            inner_matrix,
-            inner_bias,
-            outer_matrix,
-            outer_bias,
-            second_scale,
-            second_offset,
-        ),
-        ("ctx", "seq"),
-    )
+    finals = (
+        query_matrix,
+        keys_matrix,
+        value_matrix,
+        output_matrix,
+        query_bias,
+        value_bias,
+        output_bias,
+        first_scale,
+        first_offset,
+        inner_matrix,
+        inner_bias,
+        outer_matrix,
+        outer_bias,
+        second_scale,
+        second_offset,
+    )
+    for over in ("ctx", "seq"):
+        finals = lax.psum(finals, over)
     return (
         layer_out.astype(jnp.bfloat16).reshape(seqs, block, width),
         tokens_grad.reshape(seqs, block, width),

time: 1820 us -> 2140 us (1.18)
  blocking collectives: 417 us -> 672 us
  waiting for transfers between devices: 897 us -> 952 us
    psum x1 -> x2, blocking collectives: 356 us -> 611 us  [local(): finals = lax.psum(finals, over)]
    psum x0 -> x1, waiting for transfers between devices: none -> 48.6 us  [local(): finals = lax.psum(finals, over)]
    unnamed x89 -> x96, local copies, waits for them, and re-layouts: 312 us -> 323 us
    unnamed x21 -> x22, waiting for transfers between devices: 262 us -> 268 us
  transfers between devices with their start and end apart: 16 -> 17, of which waited for: 14 -> 15; matrix products, arithmetic and copies ran while one was open for 13% -> 11% of each run, Pallas kernels for 0% -> 0%
where the time goes in v1:
time: 2140 us; the launch traced here: 2130 us
  waiting for transfers between devices  952 us (44%)
  blocking collectives  672 us (31%)
  local copies, waits for them, and re-layouts  393 us (18%)
  matrix products  72.4 us (3%)
    psum x2, blocking collectives, local(): finals = lax.psum(finals, over)  611 us
    unnamed x96, local copies, waits for them, and re-layouts  323 us
    unnamed x22, waiting for transfers between devices  268 us
    all_gather x1, waiting for transfers between devices, local(): lax.all_gather(keys, 'ctx', axis=1, tiled=True)  167 us
    all_gather x1, waiting for transfers between devices, local(): lax.all_gather(values, 'ctx', axis=1, tiled=True)  150 us
    reduce_scatter x1, waiting for transfers between devices, local(): lax.psum_scatter(outer_matrix.astype(jnp.bfloat16), 'fsdp', scatter_dimen...  66.5 us
    reduce_scatter x1, waiting for transfers between devices, local(): lax.psum_scatter(inner_matrix.astype(jnp.bfloat16), 'fsdp', scatter_dimen...  66.5 us
    all_gather x1, waiting for transfers between devices, local(): lax.all_gather(w_outer, 'fsdp', axis=0, tiled=True)  59.5 us
  transfers between devices with their start and end apart: 17, of which 15 were waited for; matrix products, arithmetic and copies ran while one was open for 11% of the time, Pallas kernels for 0%

profile of v1, /device:TPU:0, one launch (start us, length us, event | category | flops | bytes accessed | tf_op | source)
XLA Modules:
  0.0 2128.9 jit_solution(12225661135092517761)
XLA Ops:
  15.4 23.6 %all-gather.20.cloned.1.call-done = bf16[768,768]{1,0:T(8,128)(2,1)} async-done(((bf16[384,768]{1,0:T(8,128)(2,1)}), bf16[768,768]{1,0:T(8,128)(2,1)}) %all-gather.20.cloned.1.call-update) | async-done | bytes 1179664 | tf_op jit(solution)/shard_map/all_gather | solution.py:89
  41.3 25.6 %all-gather.24.cloned.1.call-done = bf16[768,768]{1,0:T(8,128)(2,1)} async-done(((bf16[384,768]{1,0:T(8,128)(2,1)}), bf16[768,768]{1,0:T(8,128)(2,1)}) %all-gather.24.cloned.1.call-update) | async-done | bytes 1179664 | tf_op jit(solution)/shard_map/all_gather | solution.py:88
  120.5 150.1 %all-gather.32.cloned.1.call-done = bf16[4096,768]{1,0:T(8,128)(2,1)} async-done(((bf16[128,768]{1,0:T(8,128)(2,1)}), bf16[4096,768]{1,0:T(8,128)(2,1)}) %all-gather.32.cloned.1.call-update) | async-done | bytes 6291472 | tf_op jit(solution)/shard_map/all_gather | solution.py:103
  270.5 8.7 copy.44
  279.2 166.5 %all-gather.34.cloned.1.call-done = bf16[4096,768]{1,0:T(8,128)(2,1)} async-done(((bf16[128,768]{1,0:T(8,128)(2,1)}), bf16[4096,768]{1,0:T(8,128)(2,1)}) %all-gather.34.cloned.1.call-update) | async-done | bytes 6291472 | tf_op jit(solution)/shard_map/all_gather | solution.py:102
  454.4 33.8 %while.26 = (s32[]{:T(128)}, bf16[6,1,128,128]{2,3,1,0:T(8,128)(2,1)S(1)}, f32[6,1,2,128]{3,2,1,0:T(2,128)S(1)}, s32[6]{0:T(128)S(1)}, bf16[1,4096,768]{1,2,0:T(...) while((s32[]{:T(128)}, ...), condition=%wide.region_3.4_spmd, body=%wide.region_0.3_spmd.sunk | while | flops 275775232 | bytes 19079360 | solution.py:120
  490.3 49.7 %all-gather.28.cloned.1.call-done = bf16[768,3072]{1,0:T(8,128)(2,1)} async-done(((bf16[384,3072]{1,0:T(8,128)(2,1)}), bf16[768,3072]{1,0:T(8,128)(2,1)}) %all-gather.28.cloned.1.call-update) | async-done | bytes 4718608 | tf_op jit(solution)/shard_map/all_gather | solution.py:126
  548.4 59.5 %all-gather.30.cloned.1.call-done = bf16[3072,768]{1,0:T(8,128)(2,1)} async-done(((bf16[1536,768]{1,0:T(8,128)(2,1)}), bf16[3072,768]{1,0:T(8,128)(2,1)}) %all-gather.30.cloned.1.call-update) | async-done | bytes 4718608 | tf_op jit(solution)/shard_map/all_gather | solution.py:128
  619.1 72.0 %while.27 = (s32[]{:T(128)}, bf16[6,1,128,128]{2,3,1,0:T(8,128)(2,1)S(1)}, bf16[6,1,4096,128]{2,3,1,0:T(8,128)(2,1)}, bf16[6,1,4096,128]{2,3,1,0:T(8,128)(2,1)},...) while((s32[]{:T(128)}, ...), condition=%wide.region_14.15_spmd, body=%wide.region_12.14_spmd.sunk | while | flops 680558336 | bytes 47093020 | solution.py:186
  691.1 27.8 %copy.54 = bf16[6,1,4096,128]{3,1,0,2:T(2,128)(2,1)} copy(bf16[6,1,4096,128]{2,3,1,0:T(8,128)(2,1)} %get-tuple-element.112) | data formatting | bytes 12582912
  718.9 110.1 %bitcast_reduce_fusion.1 = bf16[4096,6,128]{2,1,0:T(8,128)(2,1)} fusion(bf16[6,1,4096,128]{3,1,0,2:T(2,128)(2,1)} %copy.54), kind=kLoop, calls=%fused_computation.29 | loop fusion | bytes 12582912
  836.8 27.9 %copy.56 = bf16[6,1,4096,128]{3,1,0,2:T(2,128)(2,1)} copy(bf16[6,1,4096,128]{2,3,1,0:T(8,128)(2,1)} %get-tuple-element.113) | data formatting | bytes 12582912
  864.6 110.0 %bitcast_reduce_fusion = bf16[4096,6,128]{2,1,0:T(8,128)(2,1)} fusion(bf16[6,1,4096,128]{3,1,0,2:T(2,128)(2,1)} %copy.56), kind=kLoop, calls=%fused_computation.28 | loop fusion | bytes 12582912
  995.6 21.5 %reduce-scatter.25.cloned.1.call-done = bf16[128,768]{1,0:T(8,128)(2,1)} async-done(((bf16[4096,768]{1,0:T(8,128)(2,1)}), bf16[128,768]{1,0:T(8,128)(2,1)}) %reduce-scatter.25.cloned.1.call-update) | async-done | bytes 196624
  1020.8 177.5 %reduce-scatter.27.cloned.1.call-done = bf16[128,768]{1,0:T(8,128)(2,1)} async-done(((bf16[4096,768]{1,0:T(8,128)(2,1)}), bf16[128,768]{1,0:T(8,128)(2,1)}) %reduce-scatter.27.cloned.1.call-update) | async-done | bytes 196624
  1204.3 19.7 reduce-scatter.29.cloned.1.call-done
  1225.4 26.8 %reduce-scatter.19.cloned.1.call-done = bf16[384,768]{1,0:T(8,128)(2,1)} async-done(((bf16[768,768]{1,0:T(8,128)(2,1)}), bf16[384,768]{1,0:T(8,128)(2,1)}) %reduce-scatter.19.cloned.1.call-update) | async-done | bytes 589840 | tf_op jit(solution)/shard_map/reduce_scatter | solution.py:235
  1252.2 66.5 %reduce-scatter.21.cloned.1.call-done = bf16[384,3072]{1,0:T(8,128)(2,1)} async-done(((bf16[768,3072]{1,0:T(8,128)(2,1)}), bf16[384,3072]{1,0:T(8,128)(2,1)}) %reduce-scatter.21.cloned.1.call-update) | async-done | bytes 2359312 | tf_op jit(solution)/shard_map/reduce_scatter | solution.py:253
  1318.6 66.5 %reduce-scatter.23.cloned.1.call-done = bf16[1536,768]{1,0:T(8,128)(2,1)} async-done(((bf16[3072,768]{1,0:T(8,128)(2,1)}), bf16[1536,768]{1,0:T(8,128)(2,1)}) %reduce-scatter.23.cloned.1.call-update) | async-done | bytes 2359312 | tf_op jit(solution)/shard_map/reduce_scatter | solution.py:259
  1385.3 8.6 all-reduce.12
  1394.5 18.6 reduce-scatter.31.cloned.1.call-done
  1414.5 26.8 %reduce-scatter.33.cloned.1.call-done = bf16[384,768]{1,0:T(8,128)(2,1)} async-done(((bf16[768,768]{1,0:T(8,128)(2,1)}), bf16[384,768]{1,0:T(8,128)(2,1)}) %reduce-scatter.33.cloned.1.call-update) | async-done | bytes 589840
  1442.7 607.2 %all-reduce.17 = (f32[384,768]{0,1:T(8,128)}, f32[384,768]{0,1:T(8,128)}, f32[384,768]{0,1:T(8,128)}, f32[384,768]{1,0:T(8,128)}, f32[384]{0:T(512)S(1)}, /*inde...) all-reduce(bf16[384,768]{0,1:T(8,128)(2,1)S(1)} %copy.59, ...), channel_id=1, replica_groups=mesh['ctx'=32,'seq'=2,'fsdp'=2] {'ctx'}, use_global_device_ids=true, to_apply=%region_18.19 | all-reduce | flops 3543552 | bytes 21270528 | tf_op jit(solution)/shard_map/psum | solution.py:290
  2059.0 48.6 %all-reduce.16.cloned.1.call-done = (f32[384,768]{0,1:T(8,128)}, f32[384,768]{0,1:T(8,128)}, f32[384,768]{0,1:T(8,128)}, f32[384,768]{1,0:T(8,128)}, f32[384,3072]{1,0:T(8,128)}, /*index=5*/f32[1536,768]{1,0:T(8,128)}) async-done(((f32[384,768]{0,1:T(8,128)}, f32[384,768]{0,1:T(8,128)}, f32[384,768]{0,1:T(8,128)}, f32[384,768]{1,0:T(8,128)}, f32[384,3072]{1,0:T(8,128)}, /*index=5*/f32[1536,768]{1,0:T(8,128)}), ...) | async-done | bytes 14155792 | tf_op jit(solution)/shard_map/psum | solution.py:290
  (371 shorter events, 255.9 us)
Async XLA Ops:
  7.2 31.8 %copy-start = (bf16[1,128,768]{2,1,0:T(8,128)(2,1)S(1)}, bf16[1,128,768]{2,1,0:T(8,128)(2,1)}, u32[]{:S(2)}) copy-start(bf16[1,128,768]{2,1,0:T(8,128)(2,1)} %param.21) | copy-start | bytes 589828
  7.2 31.8 %all-gather.20.cloned.1.call-start = ((), (), s32[]{:S(2)}) async-start(), calls=%async_computation.8 | async-start | bytes 1769472 | tf_op jit(solution)/shard_map/all_gather | solution.py:89
  7.9 59.0 %all-gather.24.cloned.1.call-start = ((), (), s32[]{:S(2)}) async-start(), calls=%async_computation.10 | async-start | bytes 1769472 | tf_op jit(solution)/shard_map/all_gather | solution.py:88
  8.7 110.0 %all-gather.22.cloned.1.call-start = ((), (), s32[]{:S(2)}) async-start(), calls=%async_computation.9 | async-start | bytes 1769472 | tf_op jit(solution)/shard_map/all_gather | solution.py:87
  9.4 261.1 %all-gather.32.cloned.1.call-start = ((), (), s32[]{:S(2)}) async-start(), calls=%async_computation.17 | async-start | bytes 6488064 | tf_op jit(solution)/shard_map/all_gather | solution.py:103
  41.3 404.5 %all-gather.34.cloned.1.call-start = ((), (), s32[]{:S(2)}) async-start(), calls=%async_computation.18 | async-start | bytes 6488064 | tf_op jit(solution)/shard_map/all_gather | solution.py:102
  69.2 419.0 %all-gather.26.cloned.1.call-start = ((), (), s32[]{:S(2)}) async-start(), calls=%async_computation.11 | async-start | bytes 1769472 | tf_op jit(solution)/shard_map/all_gather | solution.py:90
  69.8 470.2 %all-gather.28.cloned.1.call-start = ((), (), s32[]{:S(2)}) async-start(), calls=%async_computation.12 | async-start | bytes 7077888 | tf_op jit(solution)/shard_map/all_gather | solution.py:126
  70.6 18.6 copy-start.20
  70.6 24.5 %copy-start.21 = (bf16[384]{0:T(512)(128)(2,1)S(1)}, bf16[384]{0:T(512)(128)(2,1)}, u32[]{:S(2)}) copy-start(bf16[384]{0:T(512)(128)(2,1)} %param.31) | copy-start | bytes 2308
  70.6 30.3 %copy-start.22 = (bf16[384]{0:T(512)(128)(2,1)S(1)}, bf16[384]{0:T(512)(128)(2,1)}, u32[]{:S(2)}) copy-start(bf16[384]{0:T(512)(128)(2,1)} %param.30) | copy-start | bytes 2308
  70.6 36.2 %copy-start.23 = (bf16[384]{0:T(512)(128)(2,1)S(1)}, bf16[384]{0:T(512)(128)(2,1)}, u32[]{:S(2)}) copy-start(bf16[384]{0:T(512)(128)(2,1)} %param.36) | copy-start | bytes 2308
  70.6 42.1 %copy-start.24 = (bf16[384]{0:T(512)(128)(2,1)S(1)}, bf16[384]{0:T(512)(128)(2,1)}, u32[]{:S(2)}) copy-start(bf16[384]{0:T(512)(128)(2,1)} %param.37) | copy-start | bytes 2308
  70.7 537.2 %all-gather.30.cloned.1.call-start = ((), (), s32[]{:S(2)}) async-start(), calls=%async_computation.13 | async-start | bytes 7077888 | tf_op jit(solution)/shard_map/all_gather | solution.py:128
  71.4 945.6 %reduce-scatter.25.cloned.1.call-start = ((), (), s32[]{:S(2)}) async-start(), calls=%async_computation.19 | async-start | bytes 6488064
  488.2 60.2 %copy-start.7 = (bf16[6,1,128,128]{2,3,1,0:T(8,128)(2,1)}, bf16[6,1,128,128]{2,3,1,0:T(8,128)(2,1)S(1)}, u32[]{:S(2)}) copy-start(bf16[6,1,128,128]{2,3,1,0:T(8,128)(2,1)S(1)} %get-tuple-element.109) | copy-start | bytes 589828
  836.7 361.6 %reduce-scatter.27.cloned.1.call-start = ((), (), s32[]{:S(2)}) async-start(), calls=%async_computation.20 | async-start | bytes 6488064
  982.3 241.7 %reduce-scatter.29.cloned.1.call-start = ((), (), s32[]{:S(2)}) async-start(), calls=%async_computation.21 | async-start | bytes 1769472
  986.3 265.9 %reduce-scatter.19.cloned.1.call-start = ((), (), s32[]{:S(2)}) async-start(), calls=%async_computation.14 | async-start | bytes 1769472 | tf_op jit(solution)/shard_map/reduce_scatter | solution.py:235
  988.0 330.6 %reduce-scatter.21.cloned.1.call-start = ((), (), s32[]{:S(2)}) async-start(), calls=%async_computation.15 | async-start | bytes 7077888 | tf_op jit(solution)/shard_map/reduce_scatter | solution.py:253
  991.8 393.3 %reduce-scatter.23.cloned.1.call-start = ((), (), s32[]{:S(2)}) async-start(), calls=%async_computation.16 | async-start | bytes 7077888 | tf_op jit(solution)/shard_map/reduce_scatter | solution.py:259
  995.5 417.6 %reduce-scatter.31.cloned.1.call-start = ((), (), s32[]{:S(2)}) async-start(), calls=%async_computation.22 | async-start | bytes 1769472
  1020.8 420.5 %reduce-scatter.33.cloned.1.call-start = ((), (), s32[]{:S(2)}) async-start(), calls=%async_computation.23 | async-start | bytes 1769472
  1202.1 905.4 %all-reduce.16.cloned.1.call-start = ((), (), s32[]{:S(2)}) async-start(), calls=%async_computation.24 | async-start | bytes 28311552 | tf_op jit(solution)/shard_map/psum | solution.py:290
  (37 other events, 95.6 us)
Sparse Core Ops, SparseCore 0:
  9.7 29.2 all-gather.19
  40.6 26.2 all-gather.23
  68.6 26.3 all-gather.21
  97.1 173.4 all-gather.31
  272.6 173.1 all-gather.33
  447.3 24.7 all-gather.25
  473.7 66.2 all-gather.27
  541.6 66.1 all-gather.29
  836.8 180.1 reduce-scatter.24
  1019.3 179.0 reduce-scatter.26
  1201.3 22.6 reduce-scatter.28
  1226.9 25.2 reduce-scatter.18
  1255.2 63.4 reduce-scatter.20
  1321.6 63.4 reduce-scatter.22
  1387.9 25.2 reduce-scatter.30
  1416.0 25.2 reduce-scatter.32
  2050.0 57.4 all-reduce.15
